TPU v7x, 32 devices: a whole 2x2x4 slice. The times are simulated.
32 devices in a mesh: row: 8 (over y, x, core), col: 4 (over z).
Axes of the slice: x: 2, y: 2, z: 4, core: 2. Of those that a mesh axis runs over, the one named last changes fastest.
Arguments:
- homolog_embedding: bfloat16 [32, 1024, 64], P(('row', 'col')), may hold values from -6 to 6
- split_mapping_matrix: bfloat16 [64, 64], replicated, may hold values from -0.75 to 0.75
- couple_mapping_matrix: bfloat16 [1024, 128], replicated, may hold values from -1.5 to 1.5
- couple_offset_vector: bfloat16 [128], replicated, may hold values from -3 to 3
- incoming_adjoint_couple: bfloat16 [1024, 1024, 128], P('row', 'col'), may hold values from -0.29882812 to 0.29882812
Outputs:
- pair_delta_output: bfloat16 [1024, 1024, 128], P('row', 'col')
- alignment_gradient: bfloat16 [32, 1024, 64], P(('row', 'col'))
- out_weight_grad: float32 [1024, 128], replicated
All inputs are finite; a program needn't handle non-finite values.
Results may differ from a plain program's by a relative error of at most 0.015.
Values may be sent and summed in bfloat16 or wider, within the bound.
No kernel may reach another device: no remote copies, remote signals or barrier semaphores. Data moves between devices by JAX's collectives and lax.ppermute only.
A program may use at most 128 MiB of HBM per device.

v0:
```python
import math
import jax
import jax.numpy as jnp
from jax import lax
from jax.sharding import PartitionSpec as P


def standardize_features(homolog_embedding):
    mapped_halves = homolog_embedding.astype(jnp.float32)
    center = jnp.mean(mapped_halves, axis=-1, keepdims=True)
    spread = jnp.mean((mapped_halves - center) * (mapped_halves - center), axis=-1, keepdims=True)
    reciprocal_spread = lax.rsqrt(spread + 1e-05)
    return ((mapped_halves - center) * reciprocal_spread, reciprocal_spread)


def regroup(mapped_halves, outer_count, inner_count):
    shaped = mapped_halves.reshape((outer_count, inner_count, -1) + mapped_halves.shape[1:])
    return jnp.swapaxes(shaped, 0, 1).reshape(mapped_halves.shape)


def on_device(
    homolog_embedding,
    split_mapping_matrix,
    couple_mapping_matrix,
    couple_offset_vector,
    incoming_adjoint_couple,
):
    rows_count = lax.axis_size("row")
    cols_count = lax.axis_size("col")
    width = split_mapping_matrix.shape[1] // 2
    standardized_activations, reciprocal_spread = standardize_features(homolog_embedding)
    normalized_input = standardized_activations.astype(jnp.bfloat16)
    factors = jnp.dot(
        normalized_input, split_mapping_matrix, preferred_element_type=jnp.float32
    ).astype(jnp.bfloat16)
    left = factors[..., :width]
    right = factors[..., width:]
    left_all = lax.all_gather(left, "col", axis=0, tiled=True)
    left_panel = lax.all_to_all(left_all, "row", split_axis=1, concat_axis=0, tiled=True)
    right_all = lax.all_gather(right, "row", axis=0, tiled=True)
    right_panel = regroup(
        lax.all_to_all(right_all, "col", split_axis=1, concat_axis=0, tiled=True),
        cols_count,
        rows_count,
    )
    seq_total = left_panel.shape[0]
    rows_local = left_panel.shape[1]
    cols_local = right_panel.shape[1]
    channels = incoming_adjoint_couple.shape[2]
    step_rows = math.gcd(rows_local, 16)
    count = rows_local // step_rows
    left_blocks = left_panel.reshape(seq_total, count, step_rows, width).transpose(1, 0, 2, 3)
    cot_blocks = incoming_adjoint_couple.reshape(count, step_rows, cols_local, channels)
    bias_wide = couple_offset_vector.astype(jnp.float32)
    weight_back = couple_mapping_matrix.T

    def advance(carry, inputs):
        weight_sum, right_sum = carry
        left_block, cot_block = inputs
        outer = (
            jnp.einsum("sic,sje->ijce", left_block, right_panel, preferred_element_type=jnp.float32)
            / seq_total
        )
        flat = outer.astype(jnp.bfloat16).reshape(step_rows * cols_local, width * width)
        update = (
            jnp.dot(flat, couple_mapping_matrix, preferred_element_type=jnp.float32) + bias_wide
        ).astype(jnp.bfloat16)
        grad_rows = cot_block.reshape(step_rows * cols_local, channels)
        outer_grad = jnp.dot(grad_rows, weight_back, preferred_element_type=jnp.float32).astype(
            jnp.bfloat16
        )
        outer_grad = outer_grad.reshape(step_rows, cols_local, width, width)
        weight_sum = weight_sum + lax.dot_general(
            flat, grad_rows, (((0,), (0,)), ((), ())), preferred_element_type=jnp.float32
        )
        left_grad = (
            jnp.einsum("ijce,sje->sic", outer_grad, right_panel, preferred_element_type=jnp.float32)
            / seq_total
        )
        right_sum = (
            right_sum
            + jnp.einsum(
                "ijce,sic->sje", outer_grad, left_block, preferred_element_type=jnp.float32
            )
            / seq_total
        )
        return (
            (weight_sum, right_sum),
            (update.reshape(step_rows, cols_local, channels), left_grad),
        )

    start = (
        jnp.zeros((width * width, channels), jnp.float32),
        jnp.zeros((seq_total, cols_local, width), jnp.float32),
    )
    (weight_part, right_grad), (updates, left_grads) = lax.scan(
        advance, start, (left_blocks, cot_blocks)
    )
    pair_delta_output = updates.reshape(rows_local, cols_local, channels)
    left_grad = left_grads.transpose(1, 0, 2, 3).reshape(seq_total, rows_local, width)
    left_home = lax.all_to_all(
        left_grad.astype(jnp.bfloat16), "row", split_axis=0, concat_axis=1, tiled=True
    ).astype(left_grad.dtype)
    left_back = lax.psum_scatter(
        left_home.astype(jnp.bfloat16), "col", scatter_dimension=0, tiled=True
    )
    right_home = lax.all_to_all(
        regroup(right_grad, rows_count, cols_count).astype(jnp.bfloat16),
        "col",
        split_axis=0,
        concat_axis=1,
        tiled=True,
    )
    right_back = lax.psum_scatter(right_home, "row", scatter_dimension=0, tiled=True)
    factor_weight_gradient = lax.psum(weight_part, ("row", "col"))
    both = jnp.concatenate([left_back, right_back], axis=-1)
    normalized_gradient = jnp.dot(both, split_mapping_matrix.T, preferred_element_type=jnp.float32)
    first_factor = jnp.mean(normalized_gradient, axis=-1, keepdims=True)
    second_factor = jnp.mean(normalized_gradient * standardized_activations, axis=-1, keepdims=True)
    alignment_gradient = (
        reciprocal_spread
        * (normalized_gradient - first_factor - standardized_activations * second_factor)
    ).astype(jnp.bfloat16)
    return (pair_delta_output, alignment_gradient, factor_weight_gradient)


def solution(mesh):
    placed = (P(("row", "col"), None, None), P(), P(), P(), P("row", "col", None))
    return jax.shard_map(
        on_device,
        mesh=mesh,
        in_specs=placed,
        out_specs=(P("row", "col", None), P(("row", "col"), None, None), P()),
        check_vma=False,
    )
```

profile of v0, /device:TPU:0, one launch (start us, length us, event | category | flops | bytes accessed | tf_op | source)
XLA Modules:
  0.0 930.6 jit_solution(15135859743567451930)
XLA Ops:
  11.2 15.7 %all_gather.6 = bf16[4,1024,32]{1,2,0:T(8,128)(2,1)S(1)} all-gather(bf16[1,1024,32]{1,2,0:T(8,128)(2,1)S(1)} %get-tuple-element.172), channel_id=1, replica_groups=mesh['row'=8,'col'=4] {'col'}, dimensions={0}, use_global_device_ids=true | all-gather | bytes 327680 | tf_op jit(solution)/shard_map/all_gather | solution.py:38
  56.4 12.5 %all-to-all-done.1 = bf16[4,2,32768]{2,1,0:T(2,128)(2,1)S(1)} async-done(((bf16[4,2,32768]{2,1,0:T(2,128)(2,1)}), bf16[4,2,32768]{2,1,0:T(2,128)(2,1)S(1)}, u32[]{:S(2)}, u32[]{:S(2)}) %all-to-all-start.1) | async-done | bytes 524320 | tf_op jit(solution)/shard_map/all_to_all | solution.py:42
  74.7 679.0 %while.17 = (s32[]{:T(128)}, f32[1024,128]{1,0:T(8,128)S(1)}, f32[32,256,32]{1,0,2:T(8,128)S(1)}, bf16[8,16,256,128]{3,2,1,0:T(8,128)(2,1)}, bf16[8,32,16,32]{1,...) while((s32[]{:T(128)}, f32[1024,128]{1,0:T(8,128)S(1)}, ...), condition=%wide.region_3.4_spmd.clone, body=%wide.region_2.3_spmd.clone.sunk | while | flops 4041228288 | bytes 164564688 | solution.py:96
  113.0 12.3 %copy.105 = bf16[128,8,16,256]{3,1,2,0:T(8,128)(2,1)} copy(bf16[128,8,16,256]{3,2,1,0:T(8,128)(2,1)} %bitcast.161) | data formatting | bytes 16777216 | tf_op jit(solution)/shard_map/while
  144.8 11.4 %copy.106 = bf16[4096,1024]{0,1:T(8,128)(2,1)} copy(bf16[4096,1024]{1,0:T(8,128)(2,1)} %convolution_convert_fusion.3) | data formatting | bytes 16777216 | tf_op jit(solution)/shard_map/while/body/eval_jaxpr/convert_element_type | solution.py:69
  183.9 11.4 %copy.104 = bf16[16,256,32,32]{1,0,3,2:T(8,128)(2,1)} copy(bf16[16,256,32,32]{1,2,3,0:T(8,128)(2,1)} %fusion.77) | data formatting | bytes 16777216 | tf_op jit(solution)/shard_map/while/body/eval_jaxpr/convert_element_type | solution.py:64
  195.3 12.3 %copy.105 = bf16[128,8,16,256]{3,1,2,0:T(8,128)(2,1)} copy(bf16[128,8,16,256]{3,2,1,0:T(8,128)(2,1)} %bitcast.161) | data formatting | bytes 16777216 | tf_op jit(solution)/shard_map/while
  227.1 11.4 %copy.106 = bf16[4096,1024]{0,1:T(8,128)(2,1)} copy(bf16[4096,1024]{1,0:T(8,128)(2,1)} %convolution_convert_fusion.3) | data formatting | bytes 16777216 | tf_op jit(solution)/shard_map/while/body/eval_jaxpr/convert_element_type | solution.py:69
  277.7 12.3 %copy.105 = bf16[128,8,16,256]{3,1,2,0:T(8,128)(2,1)} copy(bf16[128,8,16,256]{3,2,1,0:T(8,128)(2,1)} %bitcast.161) | data formatting | bytes 16777216 | tf_op jit(solution)/shard_map/while
  309.5 11.4 %copy.106 = bf16[4096,1024]{0,1:T(8,128)(2,1)} copy(bf16[4096,1024]{1,0:T(8,128)(2,1)} %convolution_convert_fusion.3) | data formatting | bytes 16777216 | tf_op jit(solution)/shard_map/while/body/eval_jaxpr/convert_element_type | solution.py:69
  348.6 11.4 %copy.104 = bf16[16,256,32,32]{1,0,3,2:T(8,128)(2,1)} copy(bf16[16,256,32,32]{1,2,3,0:T(8,128)(2,1)} %fusion.77) | data formatting | bytes 16777216 | tf_op jit(solution)/shard_map/while/body/eval_jaxpr/convert_element_type | solution.py:64
  360.0 12.3 %copy.105 = bf16[128,8,16,256]{3,1,2,0:T(8,128)(2,1)} copy(bf16[128,8,16,256]{3,2,1,0:T(8,128)(2,1)} %bitcast.161) | data formatting | bytes 16777216 | tf_op jit(solution)/shard_map/while
  391.8 11.4 %copy.106 = bf16[4096,1024]{0,1:T(8,128)(2,1)} copy(bf16[4096,1024]{1,0:T(8,128)(2,1)} %convolution_convert_fusion.3) | data formatting | bytes 16777216 | tf_op jit(solution)/shard_map/while/body/eval_jaxpr/convert_element_type | solution.py:69
  442.3 12.3 %copy.105 = bf16[128,8,16,256]{3,1,2,0:T(8,128)(2,1)} copy(bf16[128,8,16,256]{3,2,1,0:T(8,128)(2,1)} %bitcast.161) | data formatting | bytes 16777216 | tf_op jit(solution)/shard_map/while
  474.1 11.4 %copy.106 = bf16[4096,1024]{0,1:T(8,128)(2,1)} copy(bf16[4096,1024]{1,0:T(8,128)(2,1)} %convolution_convert_fusion.3) | data formatting | bytes 16777216 | tf_op jit(solution)/shard_map/while/body/eval_jaxpr/convert_element_type | solution.py:69
  524.6 12.3 %copy.105 = bf16[128,8,16,256]{3,1,2,0:T(8,128)(2,1)} copy(bf16[128,8,16,256]{3,2,1,0:T(8,128)(2,1)} %bitcast.161) | data formatting | bytes 16777216 | tf_op jit(solution)/shard_map/while
  556.4 11.4 %copy.106 = bf16[4096,1024]{0,1:T(8,128)(2,1)} copy(bf16[4096,1024]{1,0:T(8,128)(2,1)} %convolution_convert_fusion.3) | data formatting | bytes 16777216 | tf_op jit(solution)/shard_map/while/body/eval_jaxpr/convert_element_type | solution.py:69
  606.9 12.3 %copy.105 = bf16[128,8,16,256]{3,1,2,0:T(8,128)(2,1)} copy(bf16[128,8,16,256]{3,2,1,0:T(8,128)(2,1)} %bitcast.161) | data formatting | bytes 16777216 | tf_op jit(solution)/shard_map/while
  638.7 11.4 %copy.106 = bf16[4096,1024]{0,1:T(8,128)(2,1)} copy(bf16[4096,1024]{1,0:T(8,128)(2,1)} %convolution_convert_fusion.3) | data formatting | bytes 16777216 | tf_op jit(solution)/shard_map/while/body/eval_jaxpr/convert_element_type | solution.py:69
  689.3 12.3 %copy.105 = bf16[128,8,16,256]{3,1,2,0:T(8,128)(2,1)} copy(bf16[128,8,16,256]{3,2,1,0:T(8,128)(2,1)} %bitcast.161) | data formatting | bytes 16777216 | tf_op jit(solution)/shard_map/while
  721.1 11.4 %copy.106 = bf16[4096,1024]{0,1:T(8,128)(2,1)} copy(bf16[4096,1024]{1,0:T(8,128)(2,1)} %convolution_convert_fusion.3) | data formatting | bytes 16777216 | tf_op jit(solution)/shard_map/while/body/eval_jaxpr/convert_element_type | solution.py:69
  772.8 16.1 %all-to-all-done.3 = bf16[32,256,32]{1,2,0:T(8,128)(2,1)S(1)} async-done(((bf16[32,256,32]{1,2,0:T(8,128)(2,1)}), bf16[32,256,32]{1,2,0:T(8,128)(2,1)S(1)}, u32[]{:S(2)}, u32[]{:S(2)}) %all-to-all-start.3) | async-done | bytes 524320 | tf_op jit(solution)/shard_map/all_to_all | solution.py:107
  794.2 37.3 %reduce-scatter.5.cloned.1.call-done = bf16[1,1024,32]{1,2,0:T(8,128)(2,1)} async-done(((bf16[8,1024,32]{1,2,0:T(8,128)(2,1)}), bf16[1,1024,32]{1,2,0:T(8,128)(2,1)}) %reduce-scatter.5.cloned.1.call-update) | async-done | bytes 65552 | tf_op jit(solution)/shard_map/reduce_scatter | solution.py:114
  833.4 87.6 %all-reduce.2.cloned.1.call-done = f32[1024,128]{1,0:T(8,128)} async-done(((f32[1024,128]{1,0:T(8,128)}), f32[1024,128]{1,0:T(8,128)}) %all-reduce.2.cloned.1.call-update) | async-done | bytes 524304 | tf_op jit(solution)/shard_map/psum | solution.py:115
  (200 shorter events, 512.4 us)
Async XLA Ops:
  8.0 45.9 %copy-start.5 = (bf16[1024,128]{1,0:T(8,128)(2,1)S(1)}, bf16[1024,128]{1,0:T(8,128)(2,1)}, u32[]{:S(2)}) copy-start(bf16[1024,128]{1,0:T(8,128)(2,1)} %param.9) | copy-start | bytes 786436
  26.8 27.3 %copy-start.11 = (bf16[128]{0:T(256)(128)(2,1)S(1)}, bf16[128]{0:T(256)(128)(2,1)}, u32[]{:S(2)}) copy-start(bf16[128]{0:T(256)(128)(2,1)} %param.10) | copy-start | bytes 772
  29.2 19.6 %all-to-all-start = ((bf16[8,2,8192]{2,1,0:T(2,128)(2,1)}), bf16[8,2,8192]{2,1,0:T(2,128)(2,1)S(1)}, u32[]{:S(2)}, u32[]{:S(2)}) async-start(bf16[8,2,8192]{2,1,0:T(2,128)(2,1)} %reshape.107), calls=%async_computation | async-start | bytes 524288 | tf_op jit(solution)/shard_map/all_to_all | solution.py:39
  48.8 20.2 %all-to-all-start.1 = ((bf16[4,2,32768]{2,1,0:T(2,128)(2,1)}), bf16[4,2,32768]{2,1,0:T(2,128)(2,1)S(1)}, u32[]{:S(2)}, u32[]{:S(2)}) async-start(bf16[4,2,32768]{2,1,0:T(2,128)(2,1)} %reshape.109), calls=%async_computation.1 | async-start | bytes 1048576 | tf_op jit(solution)/shard_map/all_to_all | solution.py:42
  55.1 19.6 %copy-start.3 = (f32[1024,128]{1,0:T(8,128)S(1)}, f32[1024,128]{1,0:T(8,128)}, u32[]{:S(2)}) copy-start(f32[1024,128]{1,0:T(8,128)} %custom-call) | copy-start | bytes 1572868
  113.0 12.3 %copy-start.6 = (bf16[1024,128]{1,0:T(8,128)(2,1)S(1)}, bf16[1024,128]{1,0:T(8,128)(2,1)}, u32[]{:S(2)}) copy-start(bf16[1024,128]{1,0:T(8,128)(2,1)} %get-tuple-element.283) | copy-start | bytes 786436 | tf_op jit(solution)/shard_map/while
  113.0 12.3 %copy-start.12 = (f32[128]{0:T(128)S(1)}, f32[128]{0:T(128)}, u32[]{:S(2)}) copy-start(f32[128]{0:T(128)} %get-tuple-element.284) | copy-start | bytes 1540 | tf_op jit(solution)/shard_map/while
  195.3 12.3 %copy-start.12 = (f32[128]{0:T(128)S(1)}, f32[128]{0:T(128)}, u32[]{:S(2)}) copy-start(f32[128]{0:T(128)} %get-tuple-element.284) | copy-start | bytes 1540 | tf_op jit(solution)/shard_map/while
  277.7 12.3 %copy-start.12 = (f32[128]{0:T(128)S(1)}, f32[128]{0:T(128)}, u32[]{:S(2)}) copy-start(f32[128]{0:T(128)} %get-tuple-element.284) | copy-start | bytes 1540 | tf_op jit(solution)/shard_map/while
  360.0 12.3 %copy-start.6 = (bf16[1024,128]{1,0:T(8,128)(2,1)S(1)}, bf16[1024,128]{1,0:T(8,128)(2,1)}, u32[]{:S(2)}) copy-start(bf16[1024,128]{1,0:T(8,128)(2,1)} %get-tuple-element.283) | copy-start | bytes 786436 | tf_op jit(solution)/shard_map/while
  360.0 12.3 %copy-start.12 = (f32[128]{0:T(128)S(1)}, f32[128]{0:T(128)}, u32[]{:S(2)}) copy-start(f32[128]{0:T(128)} %get-tuple-element.284) | copy-start | bytes 1540 | tf_op jit(solution)/shard_map/while
  442.3 12.3 %copy-start.12 = (f32[128]{0:T(128)S(1)}, f32[128]{0:T(128)}, u32[]{:S(2)}) copy-start(f32[128]{0:T(128)} %get-tuple-element.284) | copy-start | bytes 1540 | tf_op jit(solution)/shard_map/while
  524.6 12.3 %copy-start.12 = (f32[128]{0:T(128)S(1)}, f32[128]{0:T(128)}, u32[]{:S(2)}) copy-start(f32[128]{0:T(128)} %get-tuple-element.284) | copy-start | bytes 1540 | tf_op jit(solution)/shard_map/while
  606.9 12.3 %copy-start.12 = (f32[128]{0:T(128)S(1)}, f32[128]{0:T(128)}, u32[]{:S(2)}) copy-start(f32[128]{0:T(128)} %get-tuple-element.284) | copy-start | bytes 1540 | tf_op jit(solution)/shard_map/while
  689.2 12.3 %copy-start.12 = (f32[128]{0:T(128)S(1)}, f32[128]{0:T(128)}, u32[]{:S(2)}) copy-start(f32[128]{0:T(128)} %get-tuple-element.284) | copy-start | bytes 1540 | tf_op jit(solution)/shard_map/while
  753.7 36.1 %copy-start.4 = (f32[1024,128]{1,0:T(8,128)}, f32[1024,128]{1,0:T(8,128)S(1)}, u32[]{:S(2)}) copy-start(f32[1024,128]{1,0:T(8,128)S(1)} %get-tuple-element.66) | copy-start | bytes 1572868
  753.7 77.8 %copy-start.2 = (bf16[1,1024,64]{1,2,0:T(8,128)(2,1)S(1)}, bf16[1,1024,64]{1,2,0:T(8,128)(2,1)}, u32[]{:S(2)}) copy-start(bf16[1,1024,64]{1,2,0:T(8,128)(2,1)} %param.7) | copy-start | bytes 393220
  753.7 77.8 %copy-start.8 = (f32[1024]{0:T(1024)S(1)}, f32[1024]{0:T(1024)}, u32[]{:S(2)}) copy-start(f32[1024]{0:T(1024)} %copy-done.7) | copy-start | bytes 12292
  753.8 77.8 %copy-start.10 = (f32[1024]{0:T(1024)S(1)}, f32[1024]{0:T(1024)}, u32[]{:S(2)}) copy-start(f32[1024]{0:T(1024)} %copy-done.9) | copy-start | bytes 12292
  758.2 10.3 %all-to-all-start.2 = ((bf16[32,128,32]{1,2,0:T(8,128)(2,1)}), bf16[32,128,32]{1,2,0:T(8,128)(2,1)S(1)}, u32[]{:S(2)}, u32[]{:S(2)}) async-start(bf16[32,128,32]{1,2,0:T(8,128)(2,1)} %copy.67), calls=%async_computation.2 | async-start | bytes 524288 | tf_op jit(solution)/shard_map/all_to_all | solution.py:101
  768.4 20.5 %all-to-all-start.3 = ((bf16[32,256,32]{1,2,0:T(8,128)(2,1)}), bf16[32,256,32]{1,2,0:T(8,128)(2,1)S(1)}, u32[]{:S(2)}, u32[]{:S(2)}) async-start(bf16[32,256,32]{1,2,0:T(8,128)(2,1)} %bitcast.20), calls=%async_computation.4 | async-start | bytes 1048576 | tf_op jit(solution)/shard_map/all_to_all | solution.py:107
  771.9 22.3 %reduce-scatter.3.cloned.1.call-start = ((), (), s32[]{:S(2)}) async-start(), calls=%async_computation.6 | async-start | bytes 327680 | tf_op jit(solution)/shard_map/reduce_scatter | solution.py:104
  772.8 58.8 %reduce-scatter.5.cloned.1.call-start = ((), (), s32[]{:S(2)}) async-start(), calls=%async_computation.7 | async-start | bytes 589824 | tf_op jit(solution)/shard_map/reduce_scatter | solution.py:114
  789.8 131.2 %all-reduce.2.cloned.1.call-start = ((), (), s32[]{:S(2)}) async-start(), calls=%async_computation.8 | async-start | bytes 1048576 | tf_op jit(solution)/shard_map/psum | solution.py:115
  (17 other events, 146.2 us)
Sparse Core Ops, SparseCore 0:
  775.0 19.1 reduce-scatter.2
  797.9 33.6 reduce-scatter.4
Sparse Core Ops, SparseCore 1:
  795.5 125.4 all-reduce.1
where the time goes:
time: 940 us; the launch traced here: 931 us
  local copies, waits for them, and re-layouts  410 us (44%)
  matrix products  274 us (29%)
  waiting for transfers between devices  163 us (17%)
  blocking collectives  26.9 us (3%)
  loops' own time  20.7 us (2%)
  between operations  16.1 us (2%)
  starting transfers between devices  15.9 us (2%)
    while x64, local copies, waits for them, and re-layouts  176 us
    convert_element_type x8, local copies, waits for them, and re-layouts, advance(): jnp.dot(grad_rows, weight_back, preferred_element_type=jnp.float32)  91.1 us
    convert_element_type x8, local copies, waits for them, and re-layouts, advance(): outer.astype(jnp.bfloat16).reshape(step_rows * cols_local, width * width)  91 us
    psum x1, waiting for transfers between devices, on_device(): factor_weight_gradient = lax.psum(weight_part, ('row', 'col'))  87.6 us
    dot_general x8, matrix products, advance(): jnp.einsum('ijce,sic->sje', outer_grad, left_block, preferred_element_typ...  67 us
    dot_general x8, matrix products, advance(): lax.dot_general(flat, grad_rows, (((0,), (0,)), ((), ())), preferred_elem...  46.3 us
    dot_general x8, matrix products, advance(): jnp.dot(flat, couple_mapping_matrix, preferred_element_type=jnp.float32)  46.1 us
    dot_general x8, matrix products, advance(): jnp.dot(grad_rows, weight_back, preferred_element_type=jnp.float32)  44.5 us
  transfers between devices with their start and end apart: 7, of which 6 were waited for; matrix products, arithmetic and copies ran while one was open for 1% of the time, Pallas kernels for 0%

commit v1 on v0

--- a/solution.py
+++ b/solution.py
@@ -112,7 +112,9 @@
         tiled=True,
     )
     right_back = lax.psum_scatter(right_home, "row", scatter_dimension=0, tiled=True)
-    factor_weight_gradient = lax.psum(weight_part, ("row", "col"))
+    factor_weight_gradient = weight_part
+    for u in ("col", "row"):
+        factor_weight_gradient = lax.psum(factor_weight_gradient, axis_name=u)
     both = jnp.concatenate([left_back, right_back], axis=-1)
     normalized_gradient = jnp.dot(both, split_mapping_matrix.T, preferred_element_type=jnp.float32)
     first_factor = jnp.mean(normalized_gradient, axis=-1, keepdims=True)

time: 940 us -> 927 us (0.986)
  waiting for transfers between devices: 163 us -> 152 us
    psum x1 -> x2, waiting for transfers between devices: 87.6 us -> 56 us  [on_device(): factor_weight_gradient = lax.psum(factor_weight_gradient, axis_name=u)]
    reduce_scatter x1, waiting for transfers between devices: 3.85 us -> 20.6 us  [on_device(): lax.psum_scatter(left_home.astype(jnp.bfloat16), 'col', scatter_dimension...]
  transfers between devices with their start and end apart: 7 -> 8, of which waited for: 6 -> 6; matrix products, arithmetic and copies ran while one was open for 1% -> 2% of each run, Pallas kernels for 0% -> 0%
where the time goes in v1:
time: 927 us; the launch traced here: 919 us
  local copies, waits for them, and re-layouts  411 us (44%)
  matrix products  274 us (30%)
  waiting for transfers between devices  152 us (16%)
  blocking collectives  26.9 us (3%)
  loops' own time  20.7 us (2%)
  starting transfers between devices  15.9 us (2%)
  between operations  14.4 us (2%)
    while x64, local copies, waits for them, and re-layouts  176 us
    convert_element_type x8, local copies, waits for them, and re-layouts, advance(): jnp.dot(grad_rows, weight_back, preferred_element_type=jnp.float32)  91.1 us
    convert_element_type x8, local copies, waits for them, and re-layouts, advance(): outer.astype(jnp.bfloat16).reshape(step_rows * cols_local, width * width)  91 us
    dot_general x8, matrix products, advance(): jnp.einsum('ijce,sic->sje', outer_grad, left_block, preferred_element_typ...  67 us
    psum x2, waiting for transfers between devices, on_device(): factor_weight_gradient = lax.psum(factor_weight_gradient, axis_name=u)  56 us
    dot_general x8, matrix products, advance(): lax.dot_general(flat, grad_rows, (((0,), (0,)), ((), ())), preferred_elem...  46.3 us
    dot_general x8, matrix products, advance(): jnp.dot(flat, couple_mapping_matrix, preferred_element_type=jnp.float32)  46.1 us
    dot_general x8, matrix products, advance(): jnp.dot(grad_rows, weight_back, preferred_element_type=jnp.float32)  44.5 us
  transfers between devices with their start and end apart: 8, of which 6 were waited for; matrix products, arithmetic and copies ran while one was open for 2% of the time, Pallas kernels for 0%

profile of v1, /device:TPU:0, one launch (start us, length us, event | category | flops | bytes accessed | tf_op | source)
XLA Modules:
  0.0 918.6 jit_solution(17376376785419457085)
XLA Ops:
  10.4 15.7 %all_gather.6 = bf16[4,1024,32]{1,2,0:T(8,128)(2,1)S(1)} all-gather(bf16[1,1024,32]{1,2,0:T(8,128)(2,1)S(1)} %get-tuple-element.172), channel_id=1, replica_groups=mesh['row'=8,'col'=4] {'col'}, dimensions={0}, use_global_device_ids=true | all-gather | bytes 327680 | tf_op jit(solution)/shard_map/all_gather | solution.py:38
  55.6 12.5 %all-to-all-done.1 = bf16[4,2,32768]{2,1,0:T(2,128)(2,1)S(1)} async-done(((bf16[4,2,32768]{2,1,0:T(2,128)(2,1)}), bf16[4,2,32768]{2,1,0:T(2,128)(2,1)S(1)}, u32[]{:S(2)}, u32[]{:S(2)}) %all-to-all-start.1) | async-done | bytes 524320 | tf_op jit(solution)/shard_map/all_to_all | solution.py:42
  73.9 679.0 %while.17 = (s32[]{:T(128)}, f32[1024,128]{1,0:T(8,128)S(1)}, f32[32,256,32]{1,0,2:T(8,128)S(1)}, bf16[8,16,256,128]{3,2,1,0:T(8,128)(2,1)}, bf16[8,32,16,32]{1,...) while((s32[]{:T(128)}, f32[1024,128]{1,0:T(8,128)S(1)}, ...), condition=%wide.region_3.4_spmd.clone, body=%wide.region_2.3_spmd.clone.sunk | while | flops 4041228288 | bytes 164564688 | solution.py:96
  112.2 12.3 %copy.105 = bf16[128,8,16,256]{3,1,2,0:T(8,128)(2,1)} copy(bf16[128,8,16,256]{3,2,1,0:T(8,128)(2,1)} %bitcast.161) | data formatting | bytes 16777216 | tf_op jit(solution)/shard_map/while
  144.0 11.4 %copy.106 = bf16[4096,1024]{0,1:T(8,128)(2,1)} copy(bf16[4096,1024]{1,0:T(8,128)(2,1)} %convolution_convert_fusion.3) | data formatting | bytes 16777216 | tf_op jit(solution)/shard_map/while/body/eval_jaxpr/convert_element_type | solution.py:69
  194.5 12.3 %copy.105 = bf16[128,8,16,256]{3,1,2,0:T(8,128)(2,1)} copy(bf16[128,8,16,256]{3,2,1,0:T(8,128)(2,1)} %bitcast.161) | data formatting | bytes 16777216 | tf_op jit(solution)/shard_map/while
  226.3 11.4 %copy.106 = bf16[4096,1024]{0,1:T(8,128)(2,1)} copy(bf16[4096,1024]{1,0:T(8,128)(2,1)} %convolution_convert_fusion.3) | data formatting | bytes 16777216 | tf_op jit(solution)/shard_map/while/body/eval_jaxpr/convert_element_type | solution.py:69
  276.8 12.3 %copy.105 = bf16[128,8,16,256]{3,1,2,0:T(8,128)(2,1)} copy(bf16[128,8,16,256]{3,2,1,0:T(8,128)(2,1)} %bitcast.161) | data formatting | bytes 16777216 | tf_op jit(solution)/shard_map/while
  308.6 11.4 %copy.106 = bf16[4096,1024]{0,1:T(8,128)(2,1)} copy(bf16[4096,1024]{1,0:T(8,128)(2,1)} %convolution_convert_fusion.3) | data formatting | bytes 16777216 | tf_op jit(solution)/shard_map/while/body/eval_jaxpr/convert_element_type | solution.py:69
  359.1 12.3 %copy.105 = bf16[128,8,16,256]{3,1,2,0:T(8,128)(2,1)} copy(bf16[128,8,16,256]{3,2,1,0:T(8,128)(2,1)} %bitcast.161) | data formatting | bytes 16777216 | tf_op jit(solution)/shard_map/while
  390.9 11.4 %copy.106 = bf16[4096,1024]{0,1:T(8,128)(2,1)} copy(bf16[4096,1024]{1,0:T(8,128)(2,1)} %convolution_convert_fusion.3) | data formatting | bytes 16777216 | tf_op jit(solution)/shard_map/while/body/eval_jaxpr/convert_element_type | solution.py:69
  430.1 11.4 %copy.104 = bf16[16,256,32,32]{1,0,3,2:T(8,128)(2,1)} copy(bf16[16,256,32,32]{1,2,3,0:T(8,128)(2,1)} %fusion.77) | data formatting | bytes 16777216 | tf_op jit(solution)/shard_map/while/body/eval_jaxpr/convert_element_type | solution.py:64
  441.5 12.3 %copy.105 = bf16[128,8,16,256]{3,1,2,0:T(8,128)(2,1)} copy(bf16[128,8,16,256]{3,2,1,0:T(8,128)(2,1)} %bitcast.161) | data formatting | bytes 16777216 | tf_op jit(solution)/shard_map/while
  473.3 11.4 %copy.106 = bf16[4096,1024]{0,1:T(8,128)(2,1)} copy(bf16[4096,1024]{1,0:T(8,128)(2,1)} %convolution_convert_fusion.3) | data formatting | bytes 16777216 | tf_op jit(solution)/shard_map/while/body/eval_jaxpr/convert_element_type | solution.py:69
  523.8 12.3 %copy.105 = bf16[128,8,16,256]{3,1,2,0:T(8,128)(2,1)} copy(bf16[128,8,16,256]{3,2,1,0:T(8,128)(2,1)} %bitcast.161) | data formatting | bytes 16777216 | tf_op jit(solution)/shard_map/while
  555.6 11.4 %copy.106 = bf16[4096,1024]{0,1:T(8,128)(2,1)} copy(bf16[4096,1024]{1,0:T(8,128)(2,1)} %convolution_convert_fusion.3) | data formatting | bytes 16777216 | tf_op jit(solution)/shard_map/while/body/eval_jaxpr/convert_element_type | solution.py:69
  606.1 12.3 %copy.105 = bf16[128,8,16,256]{3,1,2,0:T(8,128)(2,1)} copy(bf16[128,8,16,256]{3,2,1,0:T(8,128)(2,1)} %bitcast.161) | data formatting | bytes 16777216 | tf_op jit(solution)/shard_map/while
  637.9 11.4 %copy.106 = bf16[4096,1024]{0,1:T(8,128)(2,1)} copy(bf16[4096,1024]{1,0:T(8,128)(2,1)} %convolution_convert_fusion.3) | data formatting | bytes 16777216 | tf_op jit(solution)/shard_map/while/body/eval_jaxpr/convert_element_type | solution.py:69
  688.4 12.3 %copy.105 = bf16[128,8,16,256]{3,1,2,0:T(8,128)(2,1)} copy(bf16[128,8,16,256]{3,2,1,0:T(8,128)(2,1)} %bitcast.161) | data formatting | bytes 16777216 | tf_op jit(solution)/shard_map/while
  720.2 11.4 %copy.106 = bf16[4096,1024]{0,1:T(8,128)(2,1)} copy(bf16[4096,1024]{1,0:T(8,128)(2,1)} %convolution_convert_fusion.3) | data formatting | bytes 16777216 | tf_op jit(solution)/shard_map/while/body/eval_jaxpr/convert_element_type | solution.py:69
  772.6 21.3 %all-to-all-done.3 = bf16[32,256,32]{1,2,0:T(8,128)(2,1)S(1)} async-done(((bf16[32,256,32]{1,2,0:T(8,128)(2,1)}), bf16[32,256,32]{1,2,0:T(8,128)(2,1)S(1)}, u32[]{:S(2)}, u32[]{:S(2)}) %all-to-all-start.3) | async-done | bytes 524320 | tf_op jit(solution)/shard_map/all_to_all | solution.py:107
  795.3 20.6 %reduce-scatter.3.cloned.1.call-done = bf16[1,1024,32]{1,2,0:T(8,128)(2,1)} async-done(((bf16[4,1024,32]{1,2,0:T(8,128)(2,1)}), bf16[1,1024,32]{1,2,0:T(8,128)(2,1)}) %reduce-scatter.3.cloned.1.call-update) | async-done | bytes 65552 | tf_op jit(solution)/shard_map/reduce_scatter | solution.py:104
  816.0 36.1 %reduce-scatter.5.cloned.1.call-done = bf16[1,1024,32]{1,2,0:T(8,128)(2,1)} async-done(((bf16[8,1024,32]{1,2,0:T(8,128)(2,1)}), bf16[1,1024,32]{1,2,0:T(8,128)(2,1)}) %reduce-scatter.5.cloned.1.call-update) | async-done | bytes 65552 | tf_op jit(solution)/shard_map/reduce_scatter | solution.py:114
  853.8 56.0 %all-reduce.5.cloned.1.call-done = f32[1024,128]{1,0:T(8,128)} async-done(((f32[1024,128]{1,0:T(8,128)}), f32[1024,128]{1,0:T(8,128)}) %all-reduce.5.cloned.1.call-update) | async-done | bytes 524304 | tf_op jit(solution)/shard_map/psum | solution.py:117
  (203 shorter events, 520.5 us)
Async XLA Ops:
  7.2 46.0 %copy-start.5 = (bf16[1024,128]{1,0:T(8,128)(2,1)S(1)}, bf16[1024,128]{1,0:T(8,128)(2,1)}, u32[]{:S(2)}) copy-start(bf16[1024,128]{1,0:T(8,128)(2,1)} %param.9) | copy-start | bytes 786436
  26.0 27.3 %copy-start.11 = (bf16[128]{0:T(256)(128)(2,1)S(1)}, bf16[128]{0:T(256)(128)(2,1)}, u32[]{:S(2)}) copy-start(bf16[128]{0:T(256)(128)(2,1)} %param.10) | copy-start | bytes 772
  28.4 19.6 %all-to-all-start = ((bf16[8,2,8192]{2,1,0:T(2,128)(2,1)}), bf16[8,2,8192]{2,1,0:T(2,128)(2,1)S(1)}, u32[]{:S(2)}, u32[]{:S(2)}) async-start(bf16[8,2,8192]{2,1,0:T(2,128)(2,1)} %reshape.107), calls=%async_computation | async-start | bytes 524288 | tf_op jit(solution)/shard_map/all_to_all | solution.py:39
  47.9 20.2 %all-to-all-start.1 = ((bf16[4,2,32768]{2,1,0:T(2,128)(2,1)}), bf16[4,2,32768]{2,1,0:T(2,128)(2,1)S(1)}, u32[]{:S(2)}, u32[]{:S(2)}) async-start(bf16[4,2,32768]{2,1,0:T(2,128)(2,1)} %reshape.109), calls=%async_computation.1 | async-start | bytes 1048576 | tf_op jit(solution)/shard_map/all_to_all | solution.py:42
  53.1 741.7 %all-reduce.3.cloned.1.call-start = ((), (), s32[]{:S(2)}) async-start(), calls=%async_computation.8 | async-start | bytes 1048576 | tf_op jit(solution)/shard_map/psum | solution.py:117
  54.3 19.6 %copy-start.3 = (f32[1024,128]{1,0:T(8,128)S(1)}, f32[1024,128]{1,0:T(8,128)}, u32[]{:S(2)}) copy-start(f32[1024,128]{1,0:T(8,128)} %custom-call) | copy-start | bytes 1572868
  112.2 12.3 %copy-start.6 = (bf16[1024,128]{1,0:T(8,128)(2,1)S(1)}, bf16[1024,128]{1,0:T(8,128)(2,1)}, u32[]{:S(2)}) copy-start(bf16[1024,128]{1,0:T(8,128)(2,1)} %get-tuple-element.283) | copy-start | bytes 786436 | tf_op jit(solution)/shard_map/while
  112.2 12.3 %copy-start.12 = (f32[128]{0:T(128)S(1)}, f32[128]{0:T(128)}, u32[]{:S(2)}) copy-start(f32[128]{0:T(128)} %get-tuple-element.284) | copy-start | bytes 1540 | tf_op jit(solution)/shard_map/while
  194.5 12.3 %copy-start.12 = (f32[128]{0:T(128)S(1)}, f32[128]{0:T(128)}, u32[]{:S(2)}) copy-start(f32[128]{0:T(128)} %get-tuple-element.284) | copy-start | bytes 1540 | tf_op jit(solution)/shard_map/while
  276.8 12.3 %copy-start.12 = (f32[128]{0:T(128)S(1)}, f32[128]{0:T(128)}, u32[]{:S(2)}) copy-start(f32[128]{0:T(128)} %get-tuple-element.284) | copy-start | bytes 1540 | tf_op jit(solution)/shard_map/while
  359.1 12.3 %copy-start.12 = (f32[128]{0:T(128)S(1)}, f32[128]{0:T(128)}, u32[]{:S(2)}) copy-start(f32[128]{0:T(128)} %get-tuple-element.284) | copy-start | bytes 1540 | tf_op jit(solution)/shard_map/while
  441.5 12.3 %copy-start.12 = (f32[128]{0:T(128)S(1)}, f32[128]{0:T(128)}, u32[]{:S(2)}) copy-start(f32[128]{0:T(128)} %get-tuple-element.284) | copy-start | bytes 1540 | tf_op jit(solution)/shard_map/while
  523.8 12.3 %copy-start.6 = (bf16[1024,128]{1,0:T(8,128)(2,1)S(1)}, bf16[1024,128]{1,0:T(8,128)(2,1)}, u32[]{:S(2)}) copy-start(bf16[1024,128]{1,0:T(8,128)(2,1)} %get-tuple-element.283) | copy-start | bytes 786436 | tf_op jit(solution)/shard_map/while
  523.8 12.3 %copy-start.12 = (f32[128]{0:T(128)S(1)}, f32[128]{0:T(128)}, u32[]{:S(2)}) copy-start(f32[128]{0:T(128)} %get-tuple-element.284) | copy-start | bytes 1540 | tf_op jit(solution)/shard_map/while
  606.1 12.3 %copy-start.12 = (f32[128]{0:T(128)S(1)}, f32[128]{0:T(128)}, u32[]{:S(2)}) copy-start(f32[128]{0:T(128)} %get-tuple-element.284) | copy-start | bytes 1540 | tf_op jit(solution)/shard_map/while
  688.4 12.3 %copy-start.12 = (f32[128]{0:T(128)S(1)}, f32[128]{0:T(128)}, u32[]{:S(2)}) copy-start(f32[128]{0:T(128)} %get-tuple-element.284) | copy-start | bytes 1540 | tf_op jit(solution)/shard_map/while
  752.9 99.1 %copy-start.2 = (bf16[1,1024,64]{1,2,0:T(8,128)(2,1)S(1)}, bf16[1,1024,64]{1,2,0:T(8,128)(2,1)}, u32[]{:S(2)}) copy-start(bf16[1,1024,64]{1,2,0:T(8,128)(2,1)} %param.7) | copy-start | bytes 393220
  752.9 99.1 %copy-start.8 = (f32[1024]{0:T(1024)S(1)}, f32[1024]{0:T(1024)}, u32[]{:S(2)}) copy-start(f32[1024]{0:T(1024)} %copy-done.7) | copy-start | bytes 12292
  752.9 99.1 %copy-start.10 = (f32[1024]{0:T(1024)S(1)}, f32[1024]{0:T(1024)}, u32[]{:S(2)}) copy-start(f32[1024]{0:T(1024)} %copy-done.9) | copy-start | bytes 12292
  757.9 10.3 %all-to-all-start.2 = ((bf16[32,128,32]{1,2,0:T(8,128)(2,1)}), bf16[32,128,32]{1,2,0:T(8,128)(2,1)S(1)}, u32[]{:S(2)}, u32[]{:S(2)}) async-start(bf16[32,128,32]{1,2,0:T(8,128)(2,1)} %copy.67), calls=%async_computation.2 | async-start | bytes 524288 | tf_op jit(solution)/shard_map/all_to_all | solution.py:101
  768.2 25.7 %all-to-all-start.3 = ((bf16[32,256,32]{1,2,0:T(8,128)(2,1)}), bf16[32,256,32]{1,2,0:T(8,128)(2,1)S(1)}, u32[]{:S(2)}, u32[]{:S(2)}) async-start(bf16[32,256,32]{1,2,0:T(8,128)(2,1)} %bitcast.20), calls=%async_computation.4 | async-start | bytes 1048576 | tf_op jit(solution)/shard_map/all_to_all | solution.py:107
  771.6 44.3 %reduce-scatter.3.cloned.1.call-start = ((), (), s32[]{:S(2)}) async-start(), calls=%async_computation.6 | async-start | bytes 327680 | tf_op jit(solution)/shard_map/reduce_scatter | solution.py:104
  772.5 79.5 %reduce-scatter.5.cloned.1.call-start = ((), (), s32[]{:S(2)}) async-start(), calls=%async_computation.7 | async-start | bytes 589824 | tf_op jit(solution)/shard_map/reduce_scatter | solution.py:114
  794.8 115.0 %all-reduce.5.cloned.1.call-start = ((), (), s32[]{:S(2)}) async-start(), calls=%async_computation.9 | async-start | bytes 1048576 | tf_op jit(solution)/shard_map/psum | solution.py:117
  (18 other events, 147.0 us)
Sparse Core Ops, SparseCore 0:
  753.8 40.7 all-reduce.2
  796.9 18.9 reduce-scatter.2
  819.6 32.3 reduce-scatter.4
  855.0 54.7 all-reduce.4
